TPU v7x, 32 devices: a whole 2x2x4 slice. The times are simulated.
32 devices in a mesh: lat: 4 (over y, x), lon: 8 (over z, core).
Axes of the slice: x: 2, y: 2, z: 4, core: 2. Of those that a mesh axis runs over, the one named last changes fastest.
Arguments:
- grad_rows: bfloat16 [32768, 128], P(('lat', 'lon')), may hold values from -6 to 6
- owner: int32 [32768, 1], P(('lat', 'lon')), may hold values from 0 to 31; in each aligned block of 1024 rows (0 to 1023, 1024 to 2047, ...) at most 64 rows name the same one
- lat_offset: int32 [32768], P(('lat', 'lon')), may hold values from 0 to 63
- lon_offset: int32 [32768], P(('lat', 'lon')), may hold values from 0 to 127
- position: bfloat16 [32768, 2], P(('lat', 'lon')), may hold values from 0 to 1
- live_count: int32 [32], P(('lat', 'lon')), may hold values from 512 to 1024
- features: bfloat16 [256, 1024, 128], P('lat', 'lon'), may hold values from -6 to 6
- conv_weight: bfloat16 [3, 3, 128, 128], replicated, may hold values from -0.1875 to 0.1875
Outputs:
- input_grad: bfloat16 [256, 1024, 128], P('lat', 'lon')
- weight_grad: float32 [3, 3, 128, 128], replicated
Inputs may be any that keep to these rules, and one draw needn't show every extreme that they name: `owner`: among the 1024 rows of one device no tile is named more than 64 times, a bound that some block reaches. `live_count`: entry k counts the real rows among the rows of device k, which come first.
All inputs are finite; a program needn't handle non-finite values.
Results may differ from a plain program's by a relative error of at most 0.012.
Values may be sent and summed in bfloat16 or wider, within the bound.
A program may use at most 128 MiB of HBM per device.

v0:
```python
import math
import jax
import jax.numpy as jnp
from jax import lax
from jax.sharding import PartitionSpec as P

rbf_scale = 1.5


def padded_2(cells, sides, width, closed):
    for axis, dim in sides:
        count = lax.axis_size(axis)
        ends = count if closed else count - 1
        head = lax.slice_in_dim(cells, 0, width, axis=dim)
        tail = lax.slice_in_dim(cells, cells.shape[dim] - width, cells.shape[dim], axis=dim)
        cells = jnp.concatenate(
            [
                lax.ppermute(tail, axis, [(i, (i + 1) % count) for i in range(ends)]),
                cells,
                lax.ppermute(head, axis, [((i + 1) % count, i) for i in range(ends)]),
            ],
            axis=dim,
        )
    return cells


def profile(frac):
    tap_index = jnp.arange(8).astype(frac.dtype)
    return jnp.exp(
        -jnp.square(tap_index[None, :] - 3.0 - frac[:, None]) / (2.0 * rbf_scale * rbf_scale)
    )


def clear_rim(padded):
    lat_index = lax.axis_index("lat")
    lat_count = lax.axis_size("lat")
    row_line = jnp.arange(padded.shape[0], dtype=jnp.int32)
    masked = (row_line == 0) & (lat_index == 0) | (row_line == padded.shape[0] - 1) & (
        lat_index == lat_count - 1
    )
    return jnp.where(masked[:, None, None], jnp.zeros_like(padded), padded)


def tap_matrix(offsets, weights, extent):
    tap_ints = jnp.arange(8, dtype=jnp.int32)
    cells = offsets[:, None] + tap_ints[None, :] + 1
    line = jnp.arange(extent, dtype=jnp.int32)
    picked = jnp.where(
        cells[:, :, None] == line[None, None, :], weights.astype(jnp.float32)[:, :, None], 0.0
    )
    return jnp.sum(picked, axis=1).astype(jnp.bfloat16)


def shards(grad_rows, owner, lat_offset, lon_offset, position, live_count, features, conv_weight):
    lat_total = lax.axis_size("lat")
    lon_total = lax.axis_size("lon")
    device_total = lat_total * lon_total
    row_total = grad_rows.shape[0]
    channels = grad_rows.shape[1]
    tile_lat = features.shape[0]
    tile_lon = features.shape[1]
    capacity = max(2, 2 * row_total // device_total)
    input_padded = clear_rim(padded_2(features, (("lat", 0), ("lon", 1)), 1, True))
    owner_tile = owner[:, 0]
    is_live = jnp.arange(row_total, dtype=jnp.int32) < live_count[0]
    matches = (
        (owner_tile[:, None] == jnp.arange(device_total, dtype=jnp.int32)[None, :])
        & is_live[:, None]
    ).astype(jnp.int32)
    earlier = jnp.cumsum(matches, axis=0) - matches
    slot_rank = jnp.sum(earlier * matches, axis=1)
    slot_index = jnp.where(is_live, owner_tile * capacity + slot_rank, device_total * capacity)
    outgoing = (
        jnp.zeros((device_total * capacity, channels), jnp.bfloat16)
        .at[slot_index]
        .set(grad_rows, mode="drop")
    )
    geometry = jnp.stack(
        [
            position[:, 0],
            position[:, 1],
            lat_offset.astype(jnp.bfloat16),
            lon_offset.astype(jnp.bfloat16),
        ],
        axis=1,
    )
    place_out = (
        jnp.zeros((device_total * capacity, 4), jnp.bfloat16)
        .at[slot_index]
        .set(geometry, mode="drop")
    )
    incoming, place_in = (
        lax.all_to_all(
            outgoing.reshape(device_total, capacity, channels),
            ("lat", "lon"),
            split_axis=0,
            concat_axis=0,
            tiled=True,
        ),
        lax.all_to_all(
            place_out.reshape(device_total, capacity, 4),
            ("lat", "lon"),
            split_axis=0,
            concat_axis=0,
            tiled=True,
        ),
    )
    incoming = incoming.reshape(-1, channels)
    place_in = place_in.reshape(-1, 4).astype(jnp.float32)
    padded_lat = tile_lat + 8
    padded_lon = tile_lon + 8
    slot_total = incoming.shape[0]
    block_rows = math.gcd(slot_total, 256)

    def accumulate(canvas, payload):
        rows_blk, place_blk = payload
        lat_weight = profile(place_blk[:, 0]).astype(jnp.bfloat16)
        lon_weight = profile(place_blk[:, 1]).astype(jnp.bfloat16)
        lat_matrix = tap_matrix(place_blk[:, 2].astype(jnp.int32), lat_weight, padded_lat)
        lon_matrix = tap_matrix(place_blk[:, 3].astype(jnp.int32), lon_weight, padded_lon)
        spread = (lon_matrix[:, :, None] * rows_blk[:, None, :]).reshape(
            rows_blk.shape[0], padded_lon * channels
        )
        canvas = canvas + lax.dot_general(
            lat_matrix, spread, (((0,), (0,)), ((), ())), preferred_element_type=jnp.float32
        )
        return (canvas, None)

    canvas, _ = lax.scan(
        accumulate,
        jnp.zeros((padded_lat, padded_lon * channels), jnp.float32),
        (incoming.reshape(-1, block_rows, channels), place_in.reshape(-1, block_rows, 4)),
    )
    canvas = canvas.reshape(padded_lat, padded_lon, channels)
    edge_rows = jnp.concatenate([canvas[:5], canvas[-5:]], axis=0)
    edge_rows = padded_2(edge_rows.astype(jnp.bfloat16), (("lat", 0),), 5, False).astype(
        edge_rows.dtype
    )
    inner = canvas[4:-4]
    inner = inner.at[:4].add(edge_rows[1:5]).at[-4:].add(edge_rows[15:19])
    rim_top = edge_rows[0] + canvas[3]
    rim_bottom = canvas[-4] + edge_rows[19]
    tall = jnp.concatenate([rim_top[None], inner, rim_bottom[None]], axis=0)
    side_cols = jnp.concatenate([tall[:, :5], tall[:, -5:]], axis=1)
    side_cols = padded_2(side_cols.astype(jnp.bfloat16), (("lon", 1),), 5, True).astype(
        side_cols.dtype
    )
    middle = tall[:, 4:-4]
    middle = middle.at[:, :4].add(side_cols[:, 1:5]).at[:, -4:].add(side_cols[:, 15:19])
    rim_left = side_cols[:, 0] + tall[:, 3]
    rim_right = tall[:, -4] + side_cols[:, 19]
    whole = jnp.concatenate([rim_left[:, None], middle, rim_right[:, None]], axis=1)
    grid_padded = clear_rim(whole.astype(jnp.bfloat16))
    grid_grad = grid_padded[1:-1, 1:-1]
    flat_grad = grid_grad.reshape(-1, channels)
    input_grad = jnp.zeros((tile_lat * tile_lon, channels), jnp.float32)
    weight_parts = []
    for a in range(3):
        for b in range(3):
            shifted = grid_padded[2 - a : 2 - a + tile_lat, 2 - b : 2 - b + tile_lon].reshape(
                -1, channels
            )
            input_grad = input_grad + lax.dot_general(
                shifted,
                conv_weight[a, b],
                (((1,), (1,)), ((), ())),
                preferred_element_type=jnp.float32,
            )
            window = input_padded[a : a + tile_lat, b : b + tile_lon].reshape(-1, channels)
            weight_parts.append(
                lax.dot_general(
                    window, flat_grad, (((0,), (0,)), ((), ())), preferred_element_type=jnp.float32
                )
            )
    weight_grad = lax.psum(
        jnp.stack(weight_parts).reshape(3, 3, channels, channels), ("lat", "lon")
    )
    return (input_grad.reshape(tile_lat, tile_lon, channels).astype(jnp.bfloat16), weight_grad)


def solution(mesh):
    placed = (
        P(("lat", "lon"), None),
        P(("lat", "lon"), None),
        P(("lat", "lon")),
        P(("lat", "lon")),
        P(("lat", "lon"), None),
        P(("lat", "lon")),
        P("lat", "lon", None),
        P(),
    )
    return jax.shard_map(
        shards, mesh=mesh, in_specs=placed, out_specs=(P("lat", "lon", None), P()), check_vma=False
    )
```

profile of v0, /device:TPU:0, one launch (start us, length us, event | category | flops | bytes accessed | tf_op | source)
XLA Modules:
  0.0 337.5 jit_solution(12751207130138029418)
XLA Ops:
  9.9 9.0 %reduce-window.6 = s32[32,8,128]{2,1,0:T(8,128)S(1)} reduce-window(s32[32,8,128]{2,1,0:T(8,128)S(1)} %fusion.91, s32[]{:T(128)} %constant.163.clone.1), window={size=1x1x128 pad=0_0x0_0x127_0}, to_apply=%region_0.1 | reduce-window | flops 4161536 | bytes 262148 | tf_op jit(solution)/shard_map/reduce-window
  26.1 7.3 %all-to-all-start = ((bf16[32,2,128]{2,1,0:T(2,128)(2,1)}), bf16[32,2,128]{2,1,0:T(2,128)(2,1)S(1)}, u32[]{:S(2)}, u32[]{:S(2)}) async-start(bf16[32,2,128]{2,1,0:T(2,128)(2,1)} %reshape.426), calls=%async_computation | async-start | bytes 32768 | tf_op jit(solution)/shard_map/all_to_all | solution.py:100
  33.4 4.3 %scatter_custom_fusion.1 = bf16[2048,128]{1,0:T(8,128)(2,1)} fusion(s32[1024]{0:T(1024)S(1)} %bitcast.220, bf16[1024,128]{1,0:T(8,128)(2,1)} %param.18, bf16[]{:T(256)} %constant.167.clone.1), kind=kCustom, calls=%fused_computation.79 | custom fusion | bytes 524800 | tf_op jit(solution)/shard_map/scatter | solution.py:76
  47.3 5.0 %collective-permute-done.4 = bf16[1,128,128]{2,1,0:T(8,128)(2,1)S(1)} collective-permute-done((bf16[1,128,128]{2,1,0:T(8,128)(2,1)S(1)}, bf16[1,128,128]{2,1,0:T(8,128)(2,1)S(1)}, u32[]{:S(2)}, u32[]{:S(2)}) %collective-permute-start.4) | collective-permute-done | bytes 32800 | tf_op jit(solution)/shard_map/ppermute | solution.py:18
  60.2 92.0 %while.17 = (s32[]{:T(128)}, f32[72,17408]{1,0:T(8,128)}, f32[8,256,4]{1,0,2:T(8,128)S(1)}, bf16[8,256,128]{2,1,0:T(8,128)(2,1)S(1)}, s32[]{:T(128)}, /*index=5*/s32[]{:T(128)}) while((s32[]{:T(128)}, f32[72,17408]{1,0:T(8,128)}, f32[8,256,4]{1,0,2:T(8,128)S(1)}, bf16[8,256,128]{2,1,0:T(8,128)(2,1)S(1)}, s32[]{:T(128)}, ...), condition=%wide.region_8.9_spmd.clone, body=%wide.region_5.8_spmd.clone.sunk | while | flops 649949696 | bytes 63590632 | solution.py:129
  60.7 5.2 %broadcast_multiply_fusion.2 = bf16[256,136,128]{2,1,0:T(8,128)(2,1)S(1)} fusion(bf16[256,128]{1,0:T(8,128)(2,1)S(1)} %dynamic-slice_bitcast_fusion.2, bf16[256,136]{1,0:T(8,128)(2,1)S(1)} %copy.114), kind=kLoop, calls=%fused_computation.5.clone.1 | loop fusion | flops 4456448 | bytes 9048064 | tf_op jit(solution)/shard_map/while/body/eval_jaxpr/mul | solution.py:121
  65.9 3.6 %convolution_add_fusion.10 = f32[72,17408]{1,0:T(8,128)S(1)} fusion(bf16[32,8,136,128]{3,2,1,0:T(8,128)(2,1)S(1)} %bitcast.180, f32[72,17408]{1,0:T(8,128)S(1)} %bitcast.182, pred[]{:T(512)S(6)} %compare.25, bf16[256,72]{0,1:T(8,128)(2,1)S(1)} %select_reduce_fusion.5), kind=kOutput, calls=%fused_computation.2.clone.1 | convolution fusion | flops 644235264 | bytes 18976768 | tf_op jit(solution)/shard_map/while/body/eval_jaxpr/dot_general | solution.py:124
  72.2 5.2 %broadcast_multiply_fusion.2 = bf16[256,136,128]{2,1,0:T(8,128)(2,1)S(1)} fusion(bf16[256,128]{1,0:T(8,128)(2,1)S(1)} %dynamic-slice_bitcast_fusion.2, bf16[256,136]{1,0:T(8,128)(2,1)S(1)} %copy.114), kind=kLoop, calls=%fused_computation.5.clone.1 | loop fusion | flops 4456448 | bytes 9048064 | tf_op jit(solution)/shard_map/while/body/eval_jaxpr/mul | solution.py:121
  77.4 3.6 %convolution_add_fusion.10 = f32[72,17408]{1,0:T(8,128)S(1)} fusion(bf16[32,8,136,128]{3,2,1,0:T(8,128)(2,1)S(1)} %bitcast.180, f32[72,17408]{1,0:T(8,128)S(1)} %bitcast.182, pred[]{:T(512)S(6)} %compare.25, bf16[256,72]{0,1:T(8,128)(2,1)S(1)} %select_reduce_fusion.5), kind=kOutput, calls=%fused_computation.2.clone.1 | convolution fusion | flops 644235264 | bytes 18976768 | tf_op jit(solution)/shard_map/while/body/eval_jaxpr/dot_general | solution.py:124
  83.7 5.2 %broadcast_multiply_fusion.2 = bf16[256,136,128]{2,1,0:T(8,128)(2,1)S(1)} fusion(bf16[256,128]{1,0:T(8,128)(2,1)S(1)} %dynamic-slice_bitcast_fusion.2, bf16[256,136]{1,0:T(8,128)(2,1)S(1)} %copy.114), kind=kLoop, calls=%fused_computation.5.clone.1 | loop fusion | flops 4456448 | bytes 9048064 | tf_op jit(solution)/shard_map/while/body/eval_jaxpr/mul | solution.py:121
  88.9 3.6 %convolution_add_fusion.10 = f32[72,17408]{1,0:T(8,128)S(1)} fusion(bf16[32,8,136,128]{3,2,1,0:T(8,128)(2,1)S(1)} %bitcast.180, f32[72,17408]{1,0:T(8,128)S(1)} %bitcast.182, pred[]{:T(512)S(6)} %compare.25, bf16[256,72]{0,1:T(8,128)(2,1)S(1)} %select_reduce_fusion.5), kind=kOutput, calls=%fused_computation.2.clone.1 | convolution fusion | flops 644235264 | bytes 18976768 | tf_op jit(solution)/shard_map/while/body/eval_jaxpr/dot_general | solution.py:124
  95.2 5.2 %broadcast_multiply_fusion.2 = bf16[256,136,128]{2,1,0:T(8,128)(2,1)S(1)} fusion(bf16[256,128]{1,0:T(8,128)(2,1)S(1)} %dynamic-slice_bitcast_fusion.2, bf16[256,136]{1,0:T(8,128)(2,1)S(1)} %copy.114), kind=kLoop, calls=%fused_computation.5.clone.1 | loop fusion | flops 4456448 | bytes 9048064 | tf_op jit(solution)/shard_map/while/body/eval_jaxpr/mul | solution.py:121
  100.4 3.6 %convolution_add_fusion.10 = f32[72,17408]{1,0:T(8,128)S(1)} fusion(bf16[32,8,136,128]{3,2,1,0:T(8,128)(2,1)S(1)} %bitcast.180, f32[72,17408]{1,0:T(8,128)S(1)} %bitcast.182, pred[]{:T(512)S(6)} %compare.25, bf16[256,72]{0,1:T(8,128)(2,1)S(1)} %select_reduce_fusion.5), kind=kOutput, calls=%fused_computation.2.clone.1 | convolution fusion | flops 644235264 | bytes 18976768 | tf_op jit(solution)/shard_map/while/body/eval_jaxpr/dot_general | solution.py:124
  106.7 5.2 %broadcast_multiply_fusion.2 = bf16[256,136,128]{2,1,0:T(8,128)(2,1)S(1)} fusion(bf16[256,128]{1,0:T(8,128)(2,1)S(1)} %dynamic-slice_bitcast_fusion.2, bf16[256,136]{1,0:T(8,128)(2,1)S(1)} %copy.114), kind=kLoop, calls=%fused_computation.5.clone.1 | loop fusion | flops 4456448 | bytes 9048064 | tf_op jit(solution)/shard_map/while/body/eval_jaxpr/mul | solution.py:121
  111.9 3.6 %convolution_add_fusion.10 = f32[72,17408]{1,0:T(8,128)S(1)} fusion(bf16[32,8,136,128]{3,2,1,0:T(8,128)(2,1)S(1)} %bitcast.180, f32[72,17408]{1,0:T(8,128)S(1)} %bitcast.182, pred[]{:T(512)S(6)} %compare.25, bf16[256,72]{0,1:T(8,128)(2,1)S(1)} %select_reduce_fusion.5), kind=kOutput, calls=%fused_computation.2.clone.1 | convolution fusion | flops 644235264 | bytes 18976768 | tf_op jit(solution)/shard_map/while/body/eval_jaxpr/dot_general | solution.py:124
  118.2 5.2 %broadcast_multiply_fusion.2 = bf16[256,136,128]{2,1,0:T(8,128)(2,1)S(1)} fusion(bf16[256,128]{1,0:T(8,128)(2,1)S(1)} %dynamic-slice_bitcast_fusion.2, bf16[256,136]{1,0:T(8,128)(2,1)S(1)} %copy.114), kind=kLoop, calls=%fused_computation.5.clone.1 | loop fusion | flops 4456448 | bytes 9048064 | tf_op jit(solution)/shard_map/while/body/eval_jaxpr/mul | solution.py:121
  123.4 3.6 %convolution_add_fusion.10 = f32[72,17408]{1,0:T(8,128)S(1)} fusion(bf16[32,8,136,128]{3,2,1,0:T(8,128)(2,1)S(1)} %bitcast.180, f32[72,17408]{1,0:T(8,128)S(1)} %bitcast.182, pred[]{:T(512)S(6)} %compare.25, bf16[256,72]{0,1:T(8,128)(2,1)S(1)} %select_reduce_fusion.5), kind=kOutput, calls=%fused_computation.2.clone.1 | convolution fusion | flops 644235264 | bytes 18976768 | tf_op jit(solution)/shard_map/while/body/eval_jaxpr/dot_general | solution.py:124
  129.7 5.2 %broadcast_multiply_fusion.2 = bf16[256,136,128]{2,1,0:T(8,128)(2,1)S(1)} fusion(bf16[256,128]{1,0:T(8,128)(2,1)S(1)} %dynamic-slice_bitcast_fusion.2, bf16[256,136]{1,0:T(8,128)(2,1)S(1)} %copy.114), kind=kLoop, calls=%fused_computation.5.clone.1 | loop fusion | flops 4456448 | bytes 9048064 | tf_op jit(solution)/shard_map/while/body/eval_jaxpr/mul | solution.py:121
  134.9 3.6 %convolution_add_fusion.10 = f32[72,17408]{1,0:T(8,128)S(1)} fusion(bf16[32,8,136,128]{3,2,1,0:T(8,128)(2,1)S(1)} %bitcast.180, f32[72,17408]{1,0:T(8,128)S(1)} %bitcast.182, pred[]{:T(512)S(6)} %compare.25, bf16[256,72]{0,1:T(8,128)(2,1)S(1)} %select_reduce_fusion.5), kind=kOutput, calls=%fused_computation.2.clone.1 | convolution fusion | flops 644235264 | bytes 18976768 | tf_op jit(solution)/shard_map/while/body/eval_jaxpr/dot_general | solution.py:124
  141.2 5.2 %broadcast_multiply_fusion.2 = bf16[256,136,128]{2,1,0:T(8,128)(2,1)S(1)} fusion(bf16[256,128]{1,0:T(8,128)(2,1)S(1)} %dynamic-slice_bitcast_fusion.2, bf16[256,136]{1,0:T(8,128)(2,1)S(1)} %copy.114), kind=kLoop, calls=%fused_computation.5.clone.1 | loop fusion | flops 4456448 | bytes 9048064 | tf_op jit(solution)/shard_map/while/body/eval_jaxpr/mul | solution.py:121
  146.4 3.6 %convolution_add_fusion.10 = f32[72,17408]{1,0:T(8,128)S(1)} fusion(bf16[32,8,136,128]{3,2,1,0:T(8,128)(2,1)S(1)} %bitcast.180, f32[72,17408]{1,0:T(8,128)S(1)} %bitcast.182, pred[]{:T(512)S(6)} %compare.25, bf16[256,72]{0,1:T(8,128)(2,1)S(1)} %select_reduce_fusion.5), kind=kOutput, calls=%fused_computation.2.clone.1 | convolution fusion | flops 644235264 | bytes 18976768 | tf_op jit(solution)/shard_map/while/body/eval_jaxpr/dot_general | solution.py:124
  160.1 4.6 %collective-permute-start = (bf16[5,136,128]{2,1,0:T(8,128)(2,1)S(1)}, bf16[5,136,128]{2,1,0:T(8,128)(2,1)S(1)}, u32[]{:S(2)}, u32[]{:S(2)}) collective-permute-start(bf16[5,136,128]{2,1,0:T(8,128)(2,1)S(1)} %bitcast.193), channel_id=1, source_target_pairs={{0,8},{8,16},{16,24},{1,9},{9,17},{17,25},{2,10},{10,18},{18,26},{... | collective-permute-start | bytes 522248 | tf_op jit(solution)/shard_map/ppermute | solution.py:18
  179.5 7.0 %fusion.126 = (bf16[64,128,128]{2,1,0:T(8,128)(2,1)}, bf16[64,128,128]{2,1,0:T(8,128)(2,1)S(1)}, bf16[64,128,128]{2,1,0:T(8,128)(2,1)}, bf16[64,128,128]{2,1,0:T...) fusion(bf16[66,130,128]{2,1,0:T(8,128)(2,1)S(1)} %get-tuple-ele, ...), kind=kLoop, calls=%fused_computation.152 | loop fusion | bytes 37748736 | tf_op jit(solution)/shard_map/slice | solution.py:160
  212.8 116.0 %all-reduce.2.cloned.1.call-done = f32[3,3,128,128]{3,2,1,0:T(8,128)} async-done(((f32[3,3,128,128]{3,2,1,0:T(8,128)}), f32[3,3,128,128]{3,2,1,0:T(8,128)}) %all-reduce.2.cloned.1.call-update) | async-done | bytes 589840 | tf_op jit(solution)/shard_map/psum | solution.py:175
  (252 shorter events, 98.3 us)
Async XLA Ops:
  26.1 14.4 %all-to-all-start = ((bf16[32,2,128]{2,1,0:T(2,128)(2,1)}), bf16[32,2,128]{2,1,0:T(2,128)(2,1)S(1)}, u32[]{:S(2)}, u32[]{:S(2)}) async-start(bf16[32,2,128]{2,1,0:T(2,128)(2,1)} %reshape.426), calls=%async_computation | async-start | bytes 32768 | tf_op jit(solution)/shard_map/all_to_all | solution.py:100
  40.5 19.7 %all-to-all-start.1 = ((bf16[32,64,128]{2,1,0:T(8,128)(2,1)}), bf16[32,64,128]{2,1,0:T(8,128)(2,1)S(1)}, u32[]{:S(2)}, u32[]{:S(2)}) async-start(bf16[32,64,128]{2,1,0:T(8,128)(2,1)} %bitcast.8), calls=%async_computation.1 | async-start | bytes 1048576 | tf_op jit(solution)/shard_map/all_to_all | solution.py:93
  43.6 285.1 %all-reduce.2.cloned.1.call-start = ((), (), s32[]{:S(2)}) async-start(), calls=%async_computation.2 | async-start | bytes 1179648 | tf_op jit(solution)/shard_map/psum | solution.py:175
  44.4 9.8 %collective-permute-start.5 = (bf16[1,128,128]{2,1,0:T(8,128)(2,1)S(1)}, bf16[1,128,128]{2,1,0:T(8,128)(2,1)S(1)}, u32[]{:S(2)}, u32[]{:S(2)}) collective-permute-start(bf16[1,128,128]{2,1,0:T(8,128)(2,1)S(1)} %get-tuple-element.168), channel_id=1, source_target_pairs={{8,0},{16,8},{24,16},{0,24},{9,1},{17,9},{25,17},{1,25},{10,2},{18... | collective-permute-start | bytes 98312 | tf_op jit(solution)/shard_map/ppermute | solution.py:20
  47.1 5.2 %collective-permute-start.4 = (bf16[1,128,128]{2,1,0:T(8,128)(2,1)S(1)}, bf16[1,128,128]{2,1,0:T(8,128)(2,1)S(1)}, u32[]{:S(2)}, u32[]{:S(2)}) collective-permute-start(bf16[1,128,128]{2,1,0:T(8,128)(2,1)S(1)} %get-tuple-element.169), channel_id=1, source_target_pairs={{0,8},{8,16},{16,24},{24,0},{1,9},{9,17},{17,25},{25,1},{2,10},{10... | collective-permute-start | bytes 98312 | tf_op jit(solution)/shard_map/ppermute | solution.py:18
  54.3 122.0 %collective-permute-start.6 = (bf16[66,1,128]{2,1,0:T(2,128)(2,1)S(1)}, bf16[66,1,128]{2,1,0:T(2,128)(2,1)S(1)}, u32[]{:S(2)}, u32[]{:S(2)}) collective-permute-start(bf16[66,1,128]{2,1,0:T(2,128)(2,1)S(1)} %get-tuple-element.166), channel_id=1, source_target_pairs={{0,1},{1,2},{2,3},{3,4},{4,5},{5,6},{6,7},{7,0},{8,9},{9,10},{10,1... | collective-permute-start | bytes 50696 | tf_op jit(solution)/shard_map/ppermute | solution.py:18
  54.4 121.9 %collective-permute-start.7 = (bf16[66,1,128]{2,1,0:T(2,128)(2,1)S(1)}, bf16[66,1,128]{2,1,0:T(2,128)(2,1)S(1)}, u32[]{:S(2)}, u32[]{:S(2)}) collective-permute-start(bf16[66,1,128]{2,1,0:T(2,128)(2,1)S(1)} %get-tuple-element.167), channel_id=1, source_target_pairs={{1,0},{2,1},{3,2},{4,3},{5,4},{6,5},{7,6},{0,7},{9,8},{10,9},{11,1... | collective-permute-start | bytes 50696 | tf_op jit(solution)/shard_map/ppermute | solution.py:20
  60.6 5.2 %slice-start = ((s8[5013504]{0:T(1024)(128)(4,1)}), s8[4194304]{0:T(1024)(128)(4,1)S(1)}, s32[]{:S(2)}) async-start(s8[5013504]{0:T(1024)(128)(4,1)} %bitcast.181), calls=%async_computation.3 | async-start | bytes 8388608 | tf_op jit(solution)/shard_map/while
  60.7 5.2 %slice-start.1 = ((s8[5013504]{0:T(1024)(128)(4,1)}), s8[819200]{0:T(1024)(128)(4,1)S(1)}, s32[]{:S(2)}) async-start(s8[5013504]{0:T(1024)(128)(4,1)} %bitcast.181), calls=%async_computation.4 | async-start | bytes 1638400 | tf_op jit(solution)/shard_map/while
  72.2 5.2 %slice-start = ((s8[5013504]{0:T(1024)(128)(4,1)}), s8[4194304]{0:T(1024)(128)(4,1)S(1)}, s32[]{:S(2)}) async-start(s8[5013504]{0:T(1024)(128)(4,1)} %bitcast.181), calls=%async_computation.3 | async-start | bytes 8388608 | tf_op jit(solution)/shard_map/while
  72.2 5.2 %slice-start.1 = ((s8[5013504]{0:T(1024)(128)(4,1)}), s8[819200]{0:T(1024)(128)(4,1)S(1)}, s32[]{:S(2)}) async-start(s8[5013504]{0:T(1024)(128)(4,1)} %bitcast.181), calls=%async_computation.4 | async-start | bytes 1638400 | tf_op jit(solution)/shard_map/while
  83.7 5.2 %slice-start = ((s8[5013504]{0:T(1024)(128)(4,1)}), s8[4194304]{0:T(1024)(128)(4,1)S(1)}, s32[]{:S(2)}) async-start(s8[5013504]{0:T(1024)(128)(4,1)} %bitcast.181), calls=%async_computation.3 | async-start | bytes 8388608 | tf_op jit(solution)/shard_map/while
  83.7 5.2 %slice-start.1 = ((s8[5013504]{0:T(1024)(128)(4,1)}), s8[819200]{0:T(1024)(128)(4,1)S(1)}, s32[]{:S(2)}) async-start(s8[5013504]{0:T(1024)(128)(4,1)} %bitcast.181), calls=%async_computation.4 | async-start | bytes 1638400 | tf_op jit(solution)/shard_map/while
  95.2 5.2 %slice-start = ((s8[5013504]{0:T(1024)(128)(4,1)}), s8[4194304]{0:T(1024)(128)(4,1)S(1)}, s32[]{:S(2)}) async-start(s8[5013504]{0:T(1024)(128)(4,1)} %bitcast.181), calls=%async_computation.3 | async-start | bytes 8388608 | tf_op jit(solution)/shard_map/while
  95.2 5.2 %slice-start.1 = ((s8[5013504]{0:T(1024)(128)(4,1)}), s8[819200]{0:T(1024)(128)(4,1)S(1)}, s32[]{:S(2)}) async-start(s8[5013504]{0:T(1024)(128)(4,1)} %bitcast.181), calls=%async_computation.4 | async-start | bytes 1638400 | tf_op jit(solution)/shard_map/while
  106.7 5.2 %slice-start = ((s8[5013504]{0:T(1024)(128)(4,1)}), s8[4194304]{0:T(1024)(128)(4,1)S(1)}, s32[]{:S(2)}) async-start(s8[5013504]{0:T(1024)(128)(4,1)} %bitcast.181), calls=%async_computation.3 | async-start | bytes 8388608 | tf_op jit(solution)/shard_map/while
  106.7 5.2 %slice-start.1 = ((s8[5013504]{0:T(1024)(128)(4,1)}), s8[819200]{0:T(1024)(128)(4,1)S(1)}, s32[]{:S(2)}) async-start(s8[5013504]{0:T(1024)(128)(4,1)} %bitcast.181), calls=%async_computation.4 | async-start | bytes 1638400 | tf_op jit(solution)/shard_map/while
  118.2 5.2 %slice-start = ((s8[5013504]{0:T(1024)(128)(4,1)}), s8[4194304]{0:T(1024)(128)(4,1)S(1)}, s32[]{:S(2)}) async-start(s8[5013504]{0:T(1024)(128)(4,1)} %bitcast.181), calls=%async_computation.3 | async-start | bytes 8388608 | tf_op jit(solution)/shard_map/while
  129.7 5.2 %slice-start = ((s8[5013504]{0:T(1024)(128)(4,1)}), s8[4194304]{0:T(1024)(128)(4,1)S(1)}, s32[]{:S(2)}) async-start(s8[5013504]{0:T(1024)(128)(4,1)} %bitcast.181), calls=%async_computation.3 | async-start | bytes 8388608 | tf_op jit(solution)/shard_map/while
  141.2 5.2 %slice-start = ((s8[5013504]{0:T(1024)(128)(4,1)}), s8[4194304]{0:T(1024)(128)(4,1)S(1)}, s32[]{:S(2)}) async-start(s8[5013504]{0:T(1024)(128)(4,1)} %bitcast.181), calls=%async_computation.3 | async-start | bytes 8388608 | tf_op jit(solution)/shard_map/while
  158.8 8.6 %collective-permute-start.1 = (bf16[5,136,128]{2,1,0:T(8,128)(2,1)S(1)}, bf16[5,136,128]{2,1,0:T(8,128)(2,1)S(1)}, u32[]{:S(2)}, u32[]{:S(2)}) collective-permute-start(bf16[5,136,128]{2,1,0:T(8,128)(2,1)S(1)} %bitcast.197), channel_id=1, source_target_pairs={{8,0},{16,8},{24,16},{9,1},{17,9},{25,17},{10,2},{18,10},{26,18},{... | collective-permute-start | bytes 522248 | tf_op jit(solution)/shard_map/ppermute | solution.py:20
  160.1 8.2 %collective-permute-start = (bf16[5,136,128]{2,1,0:T(8,128)(2,1)S(1)}, bf16[5,136,128]{2,1,0:T(8,128)(2,1)S(1)}, u32[]{:S(2)}, u32[]{:S(2)}) collective-permute-start(bf16[5,136,128]{2,1,0:T(8,128)(2,1)S(1)} %bitcast.193), channel_id=1, source_target_pairs={{0,8},{8,16},{16,24},{1,9},{9,17},{17,25},{2,10},{10,18},{18,26},{... | collective-permute-start | bytes 522248 | tf_op jit(solution)/shard_map/ppermute | solution.py:18
  168.8 6.6 %collective-permute-start.2 = (bf16[66,5,128]{2,1,0:T(8,128)(2,1)S(1)}, bf16[66,5,128]{2,1,0:T(8,128)(2,1)S(1)}, u32[]{:S(2)}, u32[]{:S(2)}) collective-permute-start(bf16[66,5,128]{2,1,0:T(8,128)(2,1)S(1)} %get-tuple-element.164), channel_id=1, source_target_pairs={{0,1},{1,2},{2,3},{3,4},{4,5},{5,6},{6,7},{7,0},{8,9},{9,10},{10,1... | collective-permute-start | bytes 253448 | tf_op jit(solution)/shard_map/ppermute | solution.py:18
  168.9 6.5 %collective-permute-start.3 = (bf16[66,5,128]{2,1,0:T(8,128)(2,1)S(1)}, bf16[66,5,128]{2,1,0:T(8,128)(2,1)S(1)}, u32[]{:S(2)}, u32[]{:S(2)}) collective-permute-start(bf16[66,5,128]{2,1,0:T(8,128)(2,1)S(1)} %get-tuple-element.165), channel_id=1, source_target_pairs={{1,0},{2,1},{3,2},{4,3},{5,4},{6,5},{7,6},{0,7},{9,8},{10,9},{11,1... | collective-permute-start | bytes 253448 | tf_op jit(solution)/shard_map/ppermute | solution.py:20
  (21 other events, 52.6 us)
Sparse Core Ops, SparseCore 0:
  198.0 130.6 all-reduce.1
where the time goes:
time: 338 us; the launch traced here: 337 us
  waiting for transfers between devices  132 us (39%)
  other arithmetic  64.7 us (19%)
  local copies, waits for them, and re-layouts  50.3 us (15%)
  matrix products  48.7 us (14%)
  starting transfers between devices  26.1 us (8%)
  between operations  15.1 us (4%)
    psum x1, waiting for transfers between devices, shards(): lax.psum(jnp.stack(weight_parts).reshape(3, 3, channels, channels), ('lat...  116 us
    mul x8, other arithmetic, accumulate(): lon_matrix[:, :, None] * rows_blk[:, None, :]  41.4 us
    dot_general x8, matrix products, accumulate(): lax.dot_general(lat_matrix, spread, (((0,), (0,)), ((), ())), preferred_e...  28.5 us
    while x48, local copies, waits for them, and re-layouts  17.9 us
    unnamed x31, local copies, waits for them, and re-layouts  13 us
    another operation x7, other arithmetic  12.8 us
    ppermute x4, starting transfers between devices, padded_2(): lax.ppermute(head, axis, [((i + 1) % count, i) for i in range(ends)])  11 us
    dot_general x9, matrix products, shards(): lax.dot_general(window, flat_grad, (((0,), (0,)), ((), ())), preferred_el...  10.5 us
  transfers between devices with their start and end apart: 11, of which 7 were waited for; matrix products, arithmetic and copies ran while one was open for 29% of the time, Pallas kernels for 0%

commit v1 on v0

--- a/solution.py
+++ b/solution.py
@@ -173,7 +173,7 @@
                 )
             )
     weight_grad = lax.psum(
-        jnp.stack(weight_parts).reshape(3, 3, channels, channels), ("lat", "lon")
+        lax.psum(jnp.stack(weight_parts).reshape(3, 3, channels, channels), "lat"), "lon"
     )
     return (input_grad.reshape(tile_lat, tile_lon, channels).astype(jnp.bfloat16), weight_grad)
 

time: 338 us -> 315 us (0.932)
  waiting for transfers between devices: 132 us -> 104 us
  matrix products: 48.7 us -> 53.2 us
    psum x1 -> x2, waiting for transfers between devices: 116 us -> 88.8 us  [the longest x1 54.3 us: shards(): lax.psum(lax.psum(jnp.stack(weight_parts).reshape(3, 3, channels, channel...]
    dot_general x9, matrix products: 9.68 us -> 14.2 us  [shards(): lax.dot_general(shifted, conv_weight[a, b], (((1,), (1,)), ((), ())), pre...]
    unnamed x31 -> x29, local copies, waits for them, and re-layouts: 13 us -> 12.3 us
  transfers between devices with their start and end apart: 11 -> 12, of which waited for: 7 -> 8; matrix products, arithmetic and copies ran while one was open for 29% -> 33% of each run, Pallas kernels for 0% -> 0%
where the time goes in v1:
time: 315 us; the launch traced here: 314 us
  waiting for transfers between devices  104 us (33%)
  other arithmetic  64.7 us (21%)
  matrix products  53.2 us (17%)
  local copies, waits for them, and re-layouts  49.6 us (16%)
  starting transfers between devices  26.4 us (8%)
  between operations  15.1 us (5%)
    psum x1, waiting for transfers between devices, shards(): lax.psum(lax.psum(jnp.stack(weight_parts).reshape(3, 3, channels, channel...  54.3 us
    mul x8, other arithmetic, accumulate(): lon_matrix[:, :, None] * rows_blk[:, None, :]  41.4 us
    psum x1, waiting for transfers between devices, shards(): lax.psum(jnp.stack(weight_parts).reshape(3, 3, channels, channels), 'lat')  34.5 us
    dot_general x8, matrix products, accumulate(): lax.dot_general(lat_matrix, spread, (((0,), (0,)), ((), ())), preferred_e...  28.5 us
    while x48, local copies, waits for them, and re-layouts  17.8 us
    dot_general x9, matrix products, shards(): lax.dot_general(shifted, conv_weight[a, b], (((1,), (1,)), ((), ())), pre...  14.2 us
    another operation x7, other arithmetic  12.8 us
    unnamed x29, local copies, waits for them, and re-layouts  12.3 us
  transfers between devices with their start and end apart: 12, of which 8 were waited for; matrix products, arithmetic and copies ran while one was open for 33% of the time, Pallas kernels for 0%

profile of v1, /device:TPU:0, one launch (start us, length us, event | category | flops | bytes accessed | tf_op | source)
XLA Modules:
  0.0 314.5 jit_solution(12399929966287027904)
XLA Ops:
  9.9 9.0 %reduce-window.6 = s32[32,8,128]{2,1,0:T(8,128)S(1)} reduce-window(s32[32,8,128]{2,1,0:T(8,128)S(1)} %fusion.91, s32[]{:T(128)} %constant.163.clone.1), window={size=1x1x128 pad=0_0x0_0x127_0}, to_apply=%region_0.1 | reduce-window | flops 4161536 | bytes 262148 | tf_op jit(solution)/shard_map/reduce-window
  26.1 7.3 %all-to-all-start = ((bf16[32,2,128]{2,1,0:T(2,128)(2,1)}), bf16[32,2,128]{2,1,0:T(2,128)(2,1)S(1)}, u32[]{:S(2)}, u32[]{:S(2)}) async-start(bf16[32,2,128]{2,1,0:T(2,128)(2,1)} %reshape.426), calls=%async_computation | async-start | bytes 32768 | tf_op jit(solution)/shard_map/all_to_all | solution.py:100
  33.4 4.3 %scatter_custom_fusion.1 = bf16[2048,128]{1,0:T(8,128)(2,1)} fusion(s32[1024]{0:T(1024)S(1)} %bitcast.220, bf16[1024,128]{1,0:T(8,128)(2,1)} %param.18, bf16[]{:T(256)} %constant.167.clone.1), kind=kCustom, calls=%fused_computation.79 | custom fusion | bytes 524800 | tf_op jit(solution)/shard_map/scatter | solution.py:76
  47.3 5.0 %collective-permute-done.4 = bf16[1,128,128]{2,1,0:T(8,128)(2,1)S(1)} collective-permute-done((bf16[1,128,128]{2,1,0:T(8,128)(2,1)S(1)}, bf16[1,128,128]{2,1,0:T(8,128)(2,1)S(1)}, u32[]{:S(2)}, u32[]{:S(2)}) %collective-permute-start.4) | collective-permute-done | bytes 32800 | tf_op jit(solution)/shard_map/ppermute | solution.py:18
  60.2 91.9 %while.17 = (s32[]{:T(128)}, f32[72,17408]{1,0:T(8,128)}, f32[8,256,4]{1,0,2:T(8,128)S(1)}, bf16[8,256,128]{2,1,0:T(8,128)(2,1)S(1)}, s32[]{:T(128)}, /*index=5*/s32[]{:T(128)}) while((s32[]{:T(128)}, f32[72,17408]{1,0:T(8,128)}, f32[8,256,4]{1,0,2:T(8,128)S(1)}, bf16[8,256,128]{2,1,0:T(8,128)(2,1)S(1)}, s32[]{:T(128)}, ...), condition=%wide.region_8.9_spmd.clone, body=%wide.region_5.8_spmd.clone.sunk | while | flops 649949696 | bytes 63590632 | solution.py:129
  60.7 5.2 %broadcast_multiply_fusion.2 = bf16[256,136,128]{2,1,0:T(8,128)(2,1)S(1)} fusion(bf16[256,128]{1,0:T(8,128)(2,1)S(1)} %dynamic-slice_bitcast_fusion.2, bf16[256,136]{1,0:T(8,128)(2,1)S(1)} %copy.114), kind=kLoop, calls=%fused_computation.5.clone.1 | loop fusion | flops 4456448 | bytes 9048064 | tf_op jit(solution)/shard_map/while/body/eval_jaxpr/mul | solution.py:121
  65.9 3.6 %convolution_add_fusion.10 = f32[72,17408]{1,0:T(8,128)S(1)} fusion(bf16[32,8,136,128]{3,2,1,0:T(8,128)(2,1)S(1)} %bitcast.180, f32[72,17408]{1,0:T(8,128)S(1)} %bitcast.182, pred[]{:T(512)S(6)} %compare.25, bf16[256,72]{0,1:T(8,128)(2,1)S(1)} %select_reduce_fusion.5), kind=kOutput, calls=%fused_computation.2.clone.1 | convolution fusion | flops 644235264 | bytes 18976768 | tf_op jit(solution)/shard_map/while/body/eval_jaxpr/dot_general | solution.py:124
  72.2 5.2 %broadcast_multiply_fusion.2 = bf16[256,136,128]{2,1,0:T(8,128)(2,1)S(1)} fusion(bf16[256,128]{1,0:T(8,128)(2,1)S(1)} %dynamic-slice_bitcast_fusion.2, bf16[256,136]{1,0:T(8,128)(2,1)S(1)} %copy.114), kind=kLoop, calls=%fused_computation.5.clone.1 | loop fusion | flops 4456448 | bytes 9048064 | tf_op jit(solution)/shard_map/while/body/eval_jaxpr/mul | solution.py:121
  77.4 3.6 %convolution_add_fusion.10 = f32[72,17408]{1,0:T(8,128)S(1)} fusion(bf16[32,8,136,128]{3,2,1,0:T(8,128)(2,1)S(1)} %bitcast.180, f32[72,17408]{1,0:T(8,128)S(1)} %bitcast.182, pred[]{:T(512)S(6)} %compare.25, bf16[256,72]{0,1:T(8,128)(2,1)S(1)} %select_reduce_fusion.5), kind=kOutput, calls=%fused_computation.2.clone.1 | convolution fusion | flops 644235264 | bytes 18976768 | tf_op jit(solution)/shard_map/while/body/eval_jaxpr/dot_general | solution.py:124
  83.7 5.2 %broadcast_multiply_fusion.2 = bf16[256,136,128]{2,1,0:T(8,128)(2,1)S(1)} fusion(bf16[256,128]{1,0:T(8,128)(2,1)S(1)} %dynamic-slice_bitcast_fusion.2, bf16[256,136]{1,0:T(8,128)(2,1)S(1)} %copy.114), kind=kLoop, calls=%fused_computation.5.clone.1 | loop fusion | flops 4456448 | bytes 9048064 | tf_op jit(solution)/shard_map/while/body/eval_jaxpr/mul | solution.py:121
  88.9 3.6 %convolution_add_fusion.10 = f32[72,17408]{1,0:T(8,128)S(1)} fusion(bf16[32,8,136,128]{3,2,1,0:T(8,128)(2,1)S(1)} %bitcast.180, f32[72,17408]{1,0:T(8,128)S(1)} %bitcast.182, pred[]{:T(512)S(6)} %compare.25, bf16[256,72]{0,1:T(8,128)(2,1)S(1)} %select_reduce_fusion.5), kind=kOutput, calls=%fused_computation.2.clone.1 | convolution fusion | flops 644235264 | bytes 18976768 | tf_op jit(solution)/shard_map/while/body/eval_jaxpr/dot_general | solution.py:124
  95.2 5.2 %broadcast_multiply_fusion.2 = bf16[256,136,128]{2,1,0:T(8,128)(2,1)S(1)} fusion(bf16[256,128]{1,0:T(8,128)(2,1)S(1)} %dynamic-slice_bitcast_fusion.2, bf16[256,136]{1,0:T(8,128)(2,1)S(1)} %copy.114), kind=kLoop, calls=%fused_computation.5.clone.1 | loop fusion | flops 4456448 | bytes 9048064 | tf_op jit(solution)/shard_map/while/body/eval_jaxpr/mul | solution.py:121
  100.4 3.6 %convolution_add_fusion.10 = f32[72,17408]{1,0:T(8,128)S(1)} fusion(bf16[32,8,136,128]{3,2,1,0:T(8,128)(2,1)S(1)} %bitcast.180, f32[72,17408]{1,0:T(8,128)S(1)} %bitcast.182, pred[]{:T(512)S(6)} %compare.25, bf16[256,72]{0,1:T(8,128)(2,1)S(1)} %select_reduce_fusion.5), kind=kOutput, calls=%fused_computation.2.clone.1 | convolution fusion | flops 644235264 | bytes 18976768 | tf_op jit(solution)/shard_map/while/body/eval_jaxpr/dot_general | solution.py:124
  106.7 5.2 %broadcast_multiply_fusion.2 = bf16[256,136,128]{2,1,0:T(8,128)(2,1)S(1)} fusion(bf16[256,128]{1,0:T(8,128)(2,1)S(1)} %dynamic-slice_bitcast_fusion.2, bf16[256,136]{1,0:T(8,128)(2,1)S(1)} %copy.114), kind=kLoop, calls=%fused_computation.5.clone.1 | loop fusion | flops 4456448 | bytes 9048064 | tf_op jit(solution)/shard_map/while/body/eval_jaxpr/mul | solution.py:121
  118.2 5.2 %broadcast_multiply_fusion.2 = bf16[256,136,128]{2,1,0:T(8,128)(2,1)S(1)} fusion(bf16[256,128]{1,0:T(8,128)(2,1)S(1)} %dynamic-slice_bitcast_fusion.2, bf16[256,136]{1,0:T(8,128)(2,1)S(1)} %copy.114), kind=kLoop, calls=%fused_computation.5.clone.1 | loop fusion | flops 4456448 | bytes 9048064 | tf_op jit(solution)/shard_map/while/body/eval_jaxpr/mul | solution.py:121
  123.4 3.6 %convolution_add_fusion.10 = f32[72,17408]{1,0:T(8,128)S(1)} fusion(bf16[32,8,136,128]{3,2,1,0:T(8,128)(2,1)S(1)} %bitcast.180, f32[72,17408]{1,0:T(8,128)S(1)} %bitcast.182, pred[]{:T(512)S(6)} %compare.25, bf16[256,72]{0,1:T(8,128)(2,1)S(1)} %select_reduce_fusion.5), kind=kOutput, calls=%fused_computation.2.clone.1 | convolution fusion | flops 644235264 | bytes 18976768 | tf_op jit(solution)/shard_map/while/body/eval_jaxpr/dot_general | solution.py:124
  129.6 5.2 %broadcast_multiply_fusion.2 = bf16[256,136,128]{2,1,0:T(8,128)(2,1)S(1)} fusion(bf16[256,128]{1,0:T(8,128)(2,1)S(1)} %dynamic-slice_bitcast_fusion.2, bf16[256,136]{1,0:T(8,128)(2,1)S(1)} %copy.114), kind=kLoop, calls=%fused_computation.5.clone.1 | loop fusion | flops 4456448 | bytes 9048064 | tf_op jit(solution)/shard_map/while/body/eval_jaxpr/mul | solution.py:121
  134.9 3.6 %convolution_add_fusion.10 = f32[72,17408]{1,0:T(8,128)S(1)} fusion(bf16[32,8,136,128]{3,2,1,0:T(8,128)(2,1)S(1)} %bitcast.180, f32[72,17408]{1,0:T(8,128)S(1)} %bitcast.182, pred[]{:T(512)S(6)} %compare.25, bf16[256,72]{0,1:T(8,128)(2,1)S(1)} %select_reduce_fusion.5), kind=kOutput, calls=%fused_computation.2.clone.1 | convolution fusion | flops 644235264 | bytes 18976768 | tf_op jit(solution)/shard_map/while/body/eval_jaxpr/dot_general | solution.py:124
  141.1 5.2 %broadcast_multiply_fusion.2 = bf16[256,136,128]{2,1,0:T(8,128)(2,1)S(1)} fusion(bf16[256,128]{1,0:T(8,128)(2,1)S(1)} %dynamic-slice_bitcast_fusion.2, bf16[256,136]{1,0:T(8,128)(2,1)S(1)} %copy.114), kind=kLoop, calls=%fused_computation.5.clone.1 | loop fusion | flops 4456448 | bytes 9048064 | tf_op jit(solution)/shard_map/while/body/eval_jaxpr/mul | solution.py:121
  160.0 4.6 %collective-permute-start = (bf16[5,136,128]{2,1,0:T(8,128)(2,1)S(1)}, bf16[5,136,128]{2,1,0:T(8,128)(2,1)S(1)}, u32[]{:S(2)}, u32[]{:S(2)}) collective-permute-start(bf16[5,136,128]{2,1,0:T(8,128)(2,1)S(1)} %bitcast.193), channel_id=1, source_target_pairs={{0,8},{8,16},{16,24},{1,9},{9,17},{17,25},{2,10},{10,18},{18,26},{... | collective-permute-start | bytes 522248 | tf_op jit(solution)/shard_map/ppermute | solution.py:18
  179.4 7.1 %fusion.126 = (bf16[64,128,128]{2,1,0:T(8,128)(2,1)}, bf16[64,128,128]{2,1,0:T(8,128)(2,1)S(1)}, bf16[64,128,128]{2,1,0:T(8,128)(2,1)}, bf16[64,128,128]{2,1,0:T...) fusion(bf16[66,130,128]{2,1,0:T(8,128)(2,1)S(1)} %get-tuple-ele, ...), kind=kLoop, calls=%fused_computation.152 | loop fusion | bytes 37748736 | tf_op jit(solution)/shard_map/slice | solution.py:160
  212.0 34.5 %all-reduce.3.cloned.1.call-done = f32[3,3,128,128]{3,2,1,0:T(8,128)} async-done(((f32[3,3,128,128]{3,2,1,0:T(8,128)}), f32[3,3,128,128]{3,2,1,0:T(8,128)}) %all-reduce.3.cloned.1.call-update) | async-done | bytes 589840 | tf_op jit(solution)/shard_map/psum | solution.py:176
  246.5 4.8 %fusion.5 = bf16[8192,128]{1,0:T(8,128)(2,1)} fusion(f32[8192,128]{1,0:T(8,128)} %convolution_add_fusion.2, bf16[8192,128]{1,0:T(8,128)(2,1)} %bitcast.192, bf16[3,3,128,128]{3,2,1,0:T(8,128)(2,1)S(1)} %copy-done.9), kind=kOutput, calls=%fused_computation.31 | convolution fusion | flops 270532608 | bytes 8421376 | tf_op jit(solution)/shard_map/dot_general | solution.py:163
  251.4 54.3 %all-reduce.5.cloned.1.call-done = f32[3,3,128,128]{3,2,1,0:T(8,128)} async-done(((f32[3,3,128,128]{3,2,1,0:T(8,128)}), f32[3,3,128,128]{3,2,1,0:T(8,128)}) %all-reduce.5.cloned.1.call-update) | async-done | bytes 589840 | tf_op jit(solution)/shard_map/psum | solution.py:175
  (253 shorter events, 104.6 us)
Async XLA Ops:
  26.1 14.4 %all-to-all-start = ((bf16[32,2,128]{2,1,0:T(2,128)(2,1)}), bf16[32,2,128]{2,1,0:T(2,128)(2,1)S(1)}, u32[]{:S(2)}, u32[]{:S(2)}) async-start(bf16[32,2,128]{2,1,0:T(2,128)(2,1)} %reshape.426), calls=%async_computation | async-start | bytes 32768 | tf_op jit(solution)/shard_map/all_to_all | solution.py:100
  40.5 19.7 %all-to-all-start.1 = ((bf16[32,64,128]{2,1,0:T(8,128)(2,1)}), bf16[32,64,128]{2,1,0:T(8,128)(2,1)S(1)}, u32[]{:S(2)}, u32[]{:S(2)}) async-start(bf16[32,64,128]{2,1,0:T(8,128)(2,1)} %bitcast.8), calls=%async_computation.1 | async-start | bytes 1048576 | tf_op jit(solution)/shard_map/all_to_all | solution.py:93
  43.6 202.9 %all-reduce.3.cloned.1.call-start = ((), (), s32[]{:S(2)}) async-start(), calls=%async_computation.2 | async-start | bytes 1179648 | tf_op jit(solution)/shard_map/psum | solution.py:176
  44.4 9.8 %collective-permute-start.5 = (bf16[1,128,128]{2,1,0:T(8,128)(2,1)S(1)}, bf16[1,128,128]{2,1,0:T(8,128)(2,1)S(1)}, u32[]{:S(2)}, u32[]{:S(2)}) collective-permute-start(bf16[1,128,128]{2,1,0:T(8,128)(2,1)S(1)} %get-tuple-element.168), channel_id=1, source_target_pairs={{8,0},{16,8},{24,16},{0,24},{9,1},{17,9},{25,17},{1,25},{10,2},{18... | collective-permute-start | bytes 98312 | tf_op jit(solution)/shard_map/ppermute | solution.py:20
  47.1 5.2 %collective-permute-start.4 = (bf16[1,128,128]{2,1,0:T(8,128)(2,1)S(1)}, bf16[1,128,128]{2,1,0:T(8,128)(2,1)S(1)}, u32[]{:S(2)}, u32[]{:S(2)}) collective-permute-start(bf16[1,128,128]{2,1,0:T(8,128)(2,1)S(1)} %get-tuple-element.169), channel_id=1, source_target_pairs={{0,8},{8,16},{16,24},{24,0},{1,9},{9,17},{17,25},{25,1},{2,10},{10... | collective-permute-start | bytes 98312 | tf_op jit(solution)/shard_map/ppermute | solution.py:18
  54.3 121.9 %collective-permute-start.6 = (bf16[66,1,128]{2,1,0:T(2,128)(2,1)S(1)}, bf16[66,1,128]{2,1,0:T(2,128)(2,1)S(1)}, u32[]{:S(2)}, u32[]{:S(2)}) collective-permute-start(bf16[66,1,128]{2,1,0:T(2,128)(2,1)S(1)} %get-tuple-element.166), channel_id=1, source_target_pairs={{0,1},{1,2},{2,3},{3,4},{4,5},{5,6},{6,7},{7,0},{8,9},{9,10},{10,1... | collective-permute-start | bytes 50696 | tf_op jit(solution)/shard_map/ppermute | solution.py:18
  54.4 121.8 %collective-permute-start.7 = (bf16[66,1,128]{2,1,0:T(2,128)(2,1)S(1)}, bf16[66,1,128]{2,1,0:T(2,128)(2,1)S(1)}, u32[]{:S(2)}, u32[]{:S(2)}) collective-permute-start(bf16[66,1,128]{2,1,0:T(2,128)(2,1)S(1)} %get-tuple-element.167), channel_id=1, source_target_pairs={{1,0},{2,1},{3,2},{4,3},{5,4},{6,5},{7,6},{0,7},{9,8},{10,9},{11,1... | collective-permute-start | bytes 50696 | tf_op jit(solution)/shard_map/ppermute | solution.py:20
  60.6 5.2 %slice-start = ((s8[5013504]{0:T(1024)(128)(4,1)}), s8[4194304]{0:T(1024)(128)(4,1)S(1)}, s32[]{:S(2)}) async-start(s8[5013504]{0:T(1024)(128)(4,1)} %bitcast.181), calls=%async_computation.4 | async-start | bytes 8388608 | tf_op jit(solution)/shard_map/while
  60.7 5.2 %slice-start.1 = ((s8[5013504]{0:T(1024)(128)(4,1)}), s8[819200]{0:T(1024)(128)(4,1)S(1)}, s32[]{:S(2)}) async-start(s8[5013504]{0:T(1024)(128)(4,1)} %bitcast.181), calls=%async_computation.5 | async-start | bytes 1638400 | tf_op jit(solution)/shard_map/while
  72.1 5.2 %slice-start = ((s8[5013504]{0:T(1024)(128)(4,1)}), s8[4194304]{0:T(1024)(128)(4,1)S(1)}, s32[]{:S(2)}) async-start(s8[5013504]{0:T(1024)(128)(4,1)} %bitcast.181), calls=%async_computation.4 | async-start | bytes 8388608 | tf_op jit(solution)/shard_map/while
  72.2 5.2 %slice-start.1 = ((s8[5013504]{0:T(1024)(128)(4,1)}), s8[819200]{0:T(1024)(128)(4,1)S(1)}, s32[]{:S(2)}) async-start(s8[5013504]{0:T(1024)(128)(4,1)} %bitcast.181), calls=%async_computation.5 | async-start | bytes 1638400 | tf_op jit(solution)/shard_map/while
  83.6 5.2 %slice-start = ((s8[5013504]{0:T(1024)(128)(4,1)}), s8[4194304]{0:T(1024)(128)(4,1)S(1)}, s32[]{:S(2)}) async-start(s8[5013504]{0:T(1024)(128)(4,1)} %bitcast.181), calls=%async_computation.4 | async-start | bytes 8388608 | tf_op jit(solution)/shard_map/while
  83.7 5.2 %slice-start.1 = ((s8[5013504]{0:T(1024)(128)(4,1)}), s8[819200]{0:T(1024)(128)(4,1)S(1)}, s32[]{:S(2)}) async-start(s8[5013504]{0:T(1024)(128)(4,1)} %bitcast.181), calls=%async_computation.5 | async-start | bytes 1638400 | tf_op jit(solution)/shard_map/while
  95.1 5.2 %slice-start = ((s8[5013504]{0:T(1024)(128)(4,1)}), s8[4194304]{0:T(1024)(128)(4,1)S(1)}, s32[]{:S(2)}) async-start(s8[5013504]{0:T(1024)(128)(4,1)} %bitcast.181), calls=%async_computation.4 | async-start | bytes 8388608 | tf_op jit(solution)/shard_map/while
  106.6 5.2 %slice-start = ((s8[5013504]{0:T(1024)(128)(4,1)}), s8[4194304]{0:T(1024)(128)(4,1)S(1)}, s32[]{:S(2)}) async-start(s8[5013504]{0:T(1024)(128)(4,1)} %bitcast.181), calls=%async_computation.4 | async-start | bytes 8388608 | tf_op jit(solution)/shard_map/while
  106.7 5.2 %slice-start.1 = ((s8[5013504]{0:T(1024)(128)(4,1)}), s8[819200]{0:T(1024)(128)(4,1)S(1)}, s32[]{:S(2)}) async-start(s8[5013504]{0:T(1024)(128)(4,1)} %bitcast.181), calls=%async_computation.5 | async-start | bytes 1638400 | tf_op jit(solution)/shard_map/while
  118.1 5.2 %slice-start = ((s8[5013504]{0:T(1024)(128)(4,1)}), s8[4194304]{0:T(1024)(128)(4,1)S(1)}, s32[]{:S(2)}) async-start(s8[5013504]{0:T(1024)(128)(4,1)} %bitcast.181), calls=%async_computation.4 | async-start | bytes 8388608 | tf_op jit(solution)/shard_map/while
  129.6 5.2 %slice-start = ((s8[5013504]{0:T(1024)(128)(4,1)}), s8[4194304]{0:T(1024)(128)(4,1)S(1)}, s32[]{:S(2)}) async-start(s8[5013504]{0:T(1024)(128)(4,1)} %bitcast.181), calls=%async_computation.4 | async-start | bytes 8388608 | tf_op jit(solution)/shard_map/while
  141.1 5.2 %slice-start = ((s8[5013504]{0:T(1024)(128)(4,1)}), s8[4194304]{0:T(1024)(128)(4,1)S(1)}, s32[]{:S(2)}) async-start(s8[5013504]{0:T(1024)(128)(4,1)} %bitcast.181), calls=%async_computation.4 | async-start | bytes 8388608 | tf_op jit(solution)/shard_map/while
  158.7 8.6 %collective-permute-start.1 = (bf16[5,136,128]{2,1,0:T(8,128)(2,1)S(1)}, bf16[5,136,128]{2,1,0:T(8,128)(2,1)S(1)}, u32[]{:S(2)}, u32[]{:S(2)}) collective-permute-start(bf16[5,136,128]{2,1,0:T(8,128)(2,1)S(1)} %bitcast.197), channel_id=1, source_target_pairs={{8,0},{16,8},{24,16},{9,1},{17,9},{25,17},{10,2},{18,10},{26,18},{... | collective-permute-start | bytes 522248 | tf_op jit(solution)/shard_map/ppermute | solution.py:20
  160.0 8.2 %collective-permute-start = (bf16[5,136,128]{2,1,0:T(8,128)(2,1)S(1)}, bf16[5,136,128]{2,1,0:T(8,128)(2,1)S(1)}, u32[]{:S(2)}, u32[]{:S(2)}) collective-permute-start(bf16[5,136,128]{2,1,0:T(8,128)(2,1)S(1)} %bitcast.193), channel_id=1, source_target_pairs={{0,8},{8,16},{16,24},{1,9},{9,17},{17,25},{2,10},{10,18},{18,26},{... | collective-permute-start | bytes 522248 | tf_op jit(solution)/shard_map/ppermute | solution.py:18
  168.7 6.6 %collective-permute-start.2 = (bf16[66,5,128]{2,1,0:T(8,128)(2,1)S(1)}, bf16[66,5,128]{2,1,0:T(8,128)(2,1)S(1)}, u32[]{:S(2)}, u32[]{:S(2)}) collective-permute-start(bf16[66,5,128]{2,1,0:T(8,128)(2,1)S(1)} %get-tuple-element.164), channel_id=1, source_target_pairs={{0,1},{1,2},{2,3},{3,4},{4,5},{5,6},{6,7},{7,0},{8,9},{9,10},{10,1... | collective-permute-start | bytes 253448 | tf_op jit(solution)/shard_map/ppermute | solution.py:18
  168.8 6.5 %collective-permute-start.3 = (bf16[66,5,128]{2,1,0:T(8,128)(2,1)S(1)}, bf16[66,5,128]{2,1,0:T(8,128)(2,1)S(1)}, u32[]{:S(2)}, u32[]{:S(2)}) collective-permute-start(bf16[66,5,128]{2,1,0:T(8,128)(2,1)S(1)} %get-tuple-element.165), channel_id=1, source_target_pairs={{1,0},{2,1},{3,2},{4,3},{5,4},{6,5},{7,6},{0,7},{9,8},{10,9},{11,1... | collective-permute-start | bytes 253448 | tf_op jit(solution)/shard_map/ppermute | solution.py:20
  197.8 107.9 %all-reduce.5.cloned.1.call-start = ((), (), s32[]{:S(2)}) async-start(), calls=%async_computation.3 | async-start | bytes 1179648 | tf_op jit(solution)/shard_map/psum | solution.py:175
  (21 other events, 56.3 us)
Sparse Core Ops, SparseCore 0:
  198.0 48.5 all-reduce.2
  248.9 56.7 all-reduce.4
